TPU v7x, 256 devices: a whole 4x4x8 slice. The times are simulated.
256 devices in a mesh: ctx: 64 (over x, z, core), head: 4 (over y).
Axes of the slice: x: 4, y: 4, z: 8, core: 2. Of those that a mesh axis runs over, the one named last changes fastest.
Arguments:
- queries: bfloat16 [16384, 4096], P('ctx', 'head'), may hold values from -5 to 5
- keys: bfloat16 [16384, 4096], P('ctx', 'head'), may hold values from -5 to 5
- values: bfloat16 [16384, 4096], P('ctx', 'head'), may hold values from -6 to 6
- grad_out: bfloat16 [16384, 4096], P('ctx', 'head'), may hold values from -6 to 6
- cluster_ids: int32 [32, 16384, 1], P(None, ('ctx', 'head')), may hold values from 0 to 255; in each aligned block of 256 rows (0 to 255, 256 to 511, ..., all dimensions but the last counted through in order) at most 2 rows name the same one
Outputs:
- attended: bfloat16 [16384, 4096], P('ctx', 'head')
- grad_queries: bfloat16 [16384, 4096], P('ctx', 'head')
- grad_keys: bfloat16 [16384, 4096], P('ctx', 'head')
- grad_values: bfloat16 [16384, 4096], P('ctx', 'head')
Inputs may be any that keep to these rules, and one draw needn't show every extreme that they name: `cluster_ids`: for every head, among the 256 tokens of any aligned block (tokens k * 256 to (k + 1) * 256 - 1) no cluster is named more than 2 times, and in every draw some cluster of some block is named exactly 2 times.
All inputs are finite; a program needn't handle non-finite values.
Results may differ from a plain program's by a relative error of at most 0.012.
Values may be sent and summed in bfloat16 or wider, within the bound.
A program may use at most 64 MiB of HBM per device.

v0:
```python
import functools

import jax
import jax.numpy as jnp
from jax import lax
from jax.experimental import pallas as pl
from jax.experimental.pallas import tpu as pltpu
from jax.sharding import PartitionSpec as P

HEAD_DIM = 128
CLUSTERS = 256
WINDOW = 256
SLOTS = 2
NEG_LARGE = -1e30
EMPTY_KEY = 64.0
MESH = pl.DeviceIdType.MESH
SCALE = HEAD_DIM**-0.5
F32 = jnp.float32
BF16 = jnp.bfloat16


def nt(a, b):
    return lax.dot_general(a, b, (((1,), (1,)), ((), ())), preferred_element_type=F32)


def tn(a, b):
    return lax.dot_general(a, b, (((0,), (0,)), ((), ())), preferred_element_type=F32)


def nn(a, b):
    return jnp.dot(a, b, preferred_element_type=F32)


def attend(query, key, value, grad, allowed):
    scores = jnp.where(allowed, nt(query, key) * SCALE, NEG_LARGE)
    top = jnp.max(scores, axis=-1, keepdims=True)
    exps = jnp.where(allowed, jnp.exp(scores - top), 0.0)
    total = jnp.maximum(jnp.sum(exps, axis=-1, keepdims=True), 1.0)
    weights = exps * (1.0 / total)
    weights16 = weights.astype(BF16)
    attended = nn(weights16, value)
    row_dot = jnp.sum(grad.astype(F32) * attended, axis=-1, keepdims=True)
    grad_scores = (weights16.astype(F32) * (nt(grad, value) - row_dot)).astype(BF16)
    grad_query = nn(grad_scores, key) * SCALE
    grad_key = tn(grad_scores, query) * SCALE
    grad_value = tn(weights16, grad)
    return attended, grad_query, grad_key, grad_value


def kernel(
    owners, peers, heads, rows,
    q_ref, k_ref, v_ref, g_ref, ids_ref,
    out_o, out_q, out_k, out_v,
    sbuf, rbuf, bsend, brecv, halo, hsend, hrecv, win, idr, crow, ccol, tcol,
    id_sem, halo_sem, hback_sem, send_sem, recv_sem, bsend_sem, brecv_sem,
):
    me = lax.axis_index("ctx")
    my_head = lax.axis_index("head")
    nxt = lax.rem(me + 1, owners)
    prv = lax.rem(me + owners - 1, owners)
    pairs = heads // 2
    each = CLUSTERS // owners
    slot_rows = owners * SLOTS * 2 * each
    pair_rows = 2 * rows

    barrier = pltpu.get_barrier_semaphore()

    def greet(i, c):
        pl.semaphore_signal(barrier, inc=1, device_id={"ctx": lax.rem(me + i, owners)}, device_id_type=MESH)
        return c

    lax.fori_loop(1, owners, greet, 0)
    for i in range(1, peers):
        pl.semaphore_signal(barrier, inc=1, device_id={"head": lax.rem(my_head + i, peers)}, device_id_type=MESH)
    pl.semaphore_wait(barrier, owners - 1 + peers - 1)

    id_copies = []
    for i in range(1, peers):
        peer = lax.rem(my_head + i, peers)
        copy = pltpu.make_async_remote_copy(
            src_ref=ids_ref.at[peer], dst_ref=idr.at[i - 1],
            send_sem=id_sem.at[0, i - 1], recv_sem=id_sem.at[1, i - 1],
            device_id={"head": peer}, device_id_type=MESH,
        )
        copy.start()
        id_copies.append(copy)
    halo_copies = []
    for i, ref in enumerate((k_ref, v_ref)):
        copy = pltpu.make_async_remote_copy(
            src_ref=ref, dst_ref=halo.at[i], send_sem=halo_sem.at[0, i], recv_sem=halo_sem.at[1, i],
            device_id={"ctx": nxt}, device_id_type=MESH,
        )
        copy.start()
        halo_copies.append(copy)
    for copy in id_copies:
        copy.wait()
    ids = ids_ref[my_head]
    for i in range(1, peers):
        ids = ids + idr[i - 1]
    head_row = lax.broadcasted_iota(jnp.int32, (heads, rows), 0)
    spot = (ids * (1 + 36 * head_row)) & (CLUSTERS - 1)
    eye = (
        lax.broadcasted_iota(jnp.int32, (rows, rows), 0) == lax.broadcasted_iota(jnp.int32, (rows, rows), 1)
    ).astype(BF16)
    spot_t = nt(eye, spot.astype(F32).astype(BF16)).astype(jnp.int32)
    for h in range(heads):
        crow[h] = spot[h : h + 1, :]
        ccol[h] = spot_t[:, h : h + 1]

    sub_tok = lax.broadcasted_iota(jnp.int32, (rows, rows), 0)
    lane_tok = lax.broadcasted_iota(jnp.int32, (rows, rows), 1)

    def place(spots, rank, hh):
        return (spots // each) * (SLOTS * 2 * each) + rank * (2 * each) + hh * each + spots % each

    def columns(h):
        return pl.ds(pl.multiple_of(h * HEAD_DIM, HEAD_DIM), HEAD_DIM)

    def build(p, c):
        lanes, tokens = [], []
        for hh in range(2):
            h = 2 * p + hh
            row, col = crow[h], ccol[h]
            same = col == row
            rank_row = jnp.sum(jnp.where(same & (sub_tok < lane_tok), 1.0, 0.0), axis=0, keepdims=True)
            rank_col = jnp.sum(jnp.where(same & (lane_tok < sub_tok), 1.0, 0.0), axis=1, keepdims=True)
            lanes.append(place(row, rank_row.astype(jnp.int32), hh))
            tcol[h] = place(col, rank_col.astype(jnp.int32), hh)
            tokens.append(jnp.concatenate([r[:, columns(h)] for r in (q_ref, k_ref, v_ref, g_ref)], axis=1))
        lane = jnp.concatenate(lanes, axis=1)
        token = jnp.concatenate(tokens, axis=0)
        hit = lax.broadcasted_iota(jnp.int32, (slot_rows, pair_rows), 0) == lane
        one_hot = jnp.where(hit, 1.0, 0.0)
        empty = jnp.where(jnp.sum(one_hot, axis=1, keepdims=True) > 0.5, 0.0, EMPTY_KEY)
        filled = nn(one_hot.astype(BF16), token)
        key_lane = lax.broadcasted_iota(jnp.int32, (1, 4 * HEAD_DIM), 1)
        mark = jnp.where((key_lane >= HEAD_DIM) & (key_lane < 2 * HEAD_DIM), 1.0, 0.0)
        filled = filled + empty * mark
        sbuf[p] = filled.astype(BF16).reshape(owners, SLOTS, 2 * each, 4 * HEAD_DIM)

        def send(i, c):
            dst = lax.rem(me + i, owners)
            pltpu.make_async_remote_copy(
                src_ref=sbuf.at[p, dst], dst_ref=rbuf.at[p, me], send_sem=send_sem.at[p], recv_sem=recv_sem.at[p],
                device_id={"ctx": dst}, device_id_type=MESH,
            ).start()
            return c

        lax.fori_loop(1, owners, send, 0)
        pltpu.make_async_copy(sbuf.at[p, me], rbuf.at[p, me], recv_sem.at[p]).start()
        return c

    lax.fori_loop(0, pairs, build, 0)

    for copy in halo_copies:
        copy.wait()
    q_pos = lax.broadcasted_iota(jnp.int32, (rows, WINDOW + rows), 0)
    k_pos = lax.broadcasted_iota(jnp.int32, (rows, WINDOW + rows), 1) - WINDOW
    in_window = (k_pos <= q_pos) & (k_pos > q_pos - WINDOW) & (k_pos + me * rows >= 0)

    def window(h, c):
        cols = columns(h)
        key_all = jnp.concatenate([halo[0, :, cols], k_ref[:, cols]], axis=0)
        value_all = jnp.concatenate([halo[1, :, cols], v_ref[:, cols]], axis=0)
        att, gq, gk, gv = attend(q_ref[:, cols], key_all, value_all, g_ref[:, cols], in_window)
        win[0, :, cols] = att
        win[1, :, cols] = gq
        win[2, :, cols] = gk[WINDOW:]
        win[3, :, cols] = gv[WINDOW:]
        hsend[0, :, cols] = gk[:WINDOW].astype(BF16)
        hsend[1, :, cols] = gv[:WINDOW].astype(BF16)
        return c

    lax.fori_loop(0, heads, window, 0)
    back_copies = []
    for i in range(2):
        copy = pltpu.make_async_remote_copy(
            src_ref=hsend.at[i], dst_ref=hrecv.at[i], send_sem=hback_sem.at[0, i], recv_sem=hback_sem.at[1, i],
            device_id={"ctx": prv}, device_id_type=MESH,
        )
        copy.start()
        back_copies.append(copy)

    groups = 2 * each
    part = owners * groups
    p_row = lax.broadcasted_iota(jnp.int32, (part, part), 0)
    p_col = lax.broadcasted_iota(jnp.int32, (part, part), 1)
    to_group = jnp.where(p_col == (p_row % owners) * groups + p_row // owners, 1.0, 0.0).astype(BF16)
    from_group = jnp.where(p_col == (p_row % groups) * owners + p_row // groups, 1.0, 0.0).astype(BF16)
    capacity = owners * SLOTS
    a_pos = lax.broadcasted_iota(jnp.int32, (capacity, capacity), 0)
    b_pos = lax.broadcasted_iota(jnp.int32, (capacity, capacity), 1)
    causal = (b_pos % owners) * SLOTS + b_pos // owners <= (a_pos % owners) * SLOTS + a_pos // owners
    first = jnp.where(lax.broadcasted_iota(jnp.int32, (8, HEAD_DIM), 1) == 0, 1.0, 0.0).astype(BF16)

    def cluster(p, c):
        pltpu.make_async_copy(rbuf.at[p], rbuf.at[p], recv_sem.at[p]).wait()
        slots = [
            nn(to_group, rbuf[p, :, r].reshape(part, 4 * HEAD_DIM)).astype(BF16) for r in range(SLOTS)
        ]
        results = [[], []]
        for g in range(groups):
            packed = jnp.concatenate([s[g * owners : (g + 1) * owners] for s in slots], axis=0)
            query, key, value, grad = (packed[:, i * HEAD_DIM : (i + 1) * HEAD_DIM] for i in range(4))
            valid = nt(first, key)[0:1, :] < EMPTY_KEY / 2
            done = attend(query, key, value, grad, causal & valid)
            done = jnp.concatenate([d.astype(BF16) for d in done], axis=1)
            for r in range(SLOTS):
                results[r].append(done[r * owners : (r + 1) * owners])
        for r in range(SLOTS):
            back = nn(from_group, jnp.concatenate(results[r], axis=0)).astype(BF16)
            bsend[p, :, r] = back.reshape(owners, groups, 4 * HEAD_DIM)

        def send(i, c):
            dst = lax.rem(me + i, owners)
            pltpu.make_async_remote_copy(
                src_ref=bsend.at[p, dst], dst_ref=brecv.at[p, me], send_sem=bsend_sem.at[p],
                recv_sem=brecv_sem.at[p], device_id={"ctx": dst}, device_id_type=MESH,
            ).start()
            return c

        lax.fori_loop(1, owners, send, 0)
        pltpu.make_async_copy(bsend.at[p, me], brecv.at[p, me], brecv_sem.at[p]).start()
        return c

    lax.fori_loop(0, pairs, cluster, 0)

    for copy in back_copies:
        copy.wait()

    def finish(p, c):
        pltpu.make_async_copy(brecv.at[p], brecv.at[p], brecv_sem.at[p]).wait()
        target = jnp.concatenate([tcol[2 * p], tcol[2 * p + 1]], axis=0)
        hit = lax.broadcasted_iota(jnp.int32, (pair_rows, slot_rows), 1) == target
        mine = nn(jnp.where(hit, 1.0, 0.0).astype(BF16), brecv[p].reshape(slot_rows, 4 * HEAD_DIM))
        for hh in range(2):
            cols = columns(2 * p + hh)
            part_of = [mine[hh * rows : (hh + 1) * rows, i * HEAD_DIM : (i + 1) * HEAD_DIM] for i in range(4)]
            out_o[:, cols] = (win[0, :, cols] + part_of[0]).astype(BF16)
            out_q[:, cols] = (win[1, :, cols] + part_of[1]).astype(BF16)
            out_k[:, cols] = (win[2, :, cols] + hrecv[0, :, cols].astype(F32) + part_of[2]).astype(BF16)
            out_v[:, cols] = (win[3, :, cols] + hrecv[1, :, cols].astype(F32) + part_of[3]).astype(BF16)
        return c

    lax.fori_loop(0, pairs, finish, 0)

    def drain(p, c):
        pltpu.make_async_copy(sbuf.at[p, pl.ds(0, owners - 1)], sbuf.at[p, pl.ds(0, owners - 1)], send_sem.at[p]).wait()
        pltpu.make_async_copy(bsend.at[p, pl.ds(0, owners - 1)], bsend.at[p, pl.ds(0, owners - 1)], bsend_sem.at[p]).wait()
        return c

    lax.fori_loop(0, pairs, drain, 0)


def on_device(queries, keys, values, grad_out, cluster_ids):
    rows, width = queries.shape
    heads = width // HEAD_DIM
    owners = lax.axis_size("ctx")
    peers = lax.axis_size("head")
    each = CLUSTERS // owners
    share = rows // peers
    ids = cluster_ids[:, :, 0].reshape(peers, heads, share)
    spread = jnp.zeros((peers, heads, rows), jnp.int32)
    spread = lax.dynamic_update_slice_in_dim(spread, ids, lax.axis_index("head") * share, axis=2)
    pairs = heads // 2
    buffer = pltpu.VMEM((pairs, owners, SLOTS, 2 * each, 4 * HEAD_DIM), BF16)
    vmem = pl.BlockSpec(memory_space=pltpu.VMEM)
    dma = pltpu.SemaphoreType.DMA
    return pl.pallas_call(
        functools.partial(kernel, owners, peers, heads, rows),
        out_shape=[jax.ShapeDtypeStruct((rows, width), BF16)] * 4,
        in_specs=[vmem] * 5,
        out_specs=[vmem] * 4,
        scratch_shapes=[
            buffer, buffer, buffer, buffer,
            pltpu.VMEM((2, WINDOW, width), BF16),
            pltpu.VMEM((2, WINDOW, width), BF16),
            pltpu.VMEM((2, WINDOW, width), BF16),
            pltpu.VMEM((4, rows, width), F32),
            pltpu.VMEM((peers - 1, heads, rows), jnp.int32),
            pltpu.VMEM((heads, 1, rows), jnp.int32),
            pltpu.VMEM((heads, rows, 1), jnp.int32),
            pltpu.VMEM((heads, rows, 1), jnp.int32),
            dma((2, peers - 1)), dma((2, 2)), dma((2, 2)),
            dma((pairs,)), dma((pairs,)), dma((pairs,)), dma((pairs,)),
        ],
        compiler_params=pltpu.CompilerParams(
            collective_id=0, has_side_effects=True, vmem_limit_bytes=60 * 1024 * 1024
        ),
    )(queries, keys, values, grad_out, spread)


def solution(mesh):
    return jax.shard_map(
        on_device,
        mesh=mesh,
        in_specs=(
            P("ctx", "head"), P("ctx", "head"), P("ctx", "head"), P("ctx", "head"),
            P(None, ("ctx", "head"), None),
        ),
        out_specs=(P("ctx", "head"),) * 4,
        check_vma=False,
    )
```

profile of v0, /device:TPU:1, one launch (start us, length us, event | category | flops | bytes accessed | tf_op | source)
XLA Modules:
  0.0 221.1 jit_solution(15623302592385848181)
XLA Ops:
  0.6 0.0 copy-start.4
  0.7 0.7 copy-done.4
  1.4 0.1 dynamic_update_slice.3.ids_ref
  1.5 0.0 copy-start.3
  1.5 0.6 copy-done.3
  2.1 213.8 %shard_map.84 = (bf16[256,1024]{1,0:T(8,128)(2,1)}, bf16[256,1024]{1,0:T(8,128)(2,1)}, bf16[256,1024]{1,0:T(8,128)(2,1)}, bf16[256,1024]{1,0:T(8,128)(2,1)}) custom-call(bf16[256,1024]{1,0:T(8,128)(2,1)} %q_ref.1, bf16[256,1024]{1,0:T(8,128)(2,1)} %k_ref.1, bf16[256,1024]{1,0:T(8,128)(2,1)} %v_ref.1, bf16[256,1024]{1,0:T(8,128)(2,1)} %g_ref.1, ...), custom_call_target="tpu_custom_call" | custom-call | tf_op jit(solution)/shard_map/pallas_call | solution.py:269
  215.9 0.0 copy-start.2
  215.9 1.9 copy.14
  217.8 0.0 copy-done.2
  217.8 0.0 copy-start.1
  217.8 0.8 copy.15
  218.6 0.4 copy-done.1
  219.1 0.0 copy-start
  219.1 0.8 copy.16
  219.9 0.4 copy-done
  220.3 0.8 copy.17
  (1 shorter events, 0.0 us)
Async XLA Ops:
  0.6 0.7 copy-start.4
  1.5 0.6 copy-start.3
  215.9 1.9 copy-start.2
  217.8 1.2 copy-start.1
  219.1 1.2 copy-start
where the time goes:
time: 221 us
  Pallas kernels  214 us (97%)
  local copies, waits for them, and re-layouts  6.61 us (3%)
    pallas_call x1, Pallas kernels, on_device(): pl.pallas_call(functools.partial(kernel, owners, peers, heads, rows), out...  214 us
    unnamed x14, local copies, waits for them, and re-layouts  6.49 us

commit v1 on v0

--- a/solution.py
+++ b/solution.py
@@ -47,7 +47,7 @@
     return attended, grad_query, grad_key, grad_value
 
 
-def kernel(
+def wide_kernel(
     owners, peers, heads, rows,
     q_ref, k_ref, v_ref, g_ref, ids_ref,
     out_o, out_q, out_k, out_v,
@@ -252,6 +252,376 @@
     lax.fori_loop(0, pairs, drain, 0)
 
 
+TABLE = (1, 37, 91, 151, 203, 117, 173, 55)
+LINE = 8
+FIRST_CAP = 48
+NEXT_CAP = 80
+META = 128
+
+
+def kernel(
+    owners, peers, heads, rows,
+    q_ref, k_ref, v_ref, g_ref, ids_ref,
+    out_o, out_q, out_k, out_v, out_flag,
+    sbuf, rbuf, bsend, brecv, halo, hsend, hrecv, win, idr, crow, ccol, trow, tcol, erow, ecol,
+    acc, e1, r1, e2, r2, back_acc, e3, r3, e4, r4, relay_row, expand_row, flag_out, flag_y, flag_in,
+    id_sem, halo_sem, hback_sem, send_sem, recv_sem, bsend_sem, brecv_sem, e_send, e_recv, fy_sem, f_send, f_recv,
+):
+    me = lax.axis_index("ctx")
+    my_head = lax.axis_index("head")
+    nxt = lax.rem(me + 1, owners)
+    prv = lax.rem(me + owners - 1, owners)
+    my_x, my_z, my_c = me // 16, (me // 2) % LINE, me % 2
+    my_w = my_x * 2 + my_c
+    pairs = heads // 2
+    each = CLUSTERS // owners
+    groups = 2 * each
+    part = owners * groups
+    pair_rows = 2 * rows
+    wide = 4 * HEAD_DIM
+    first_rows, next_rows = LINE * FIRST_CAP, LINE * NEXT_CAP
+
+    barrier = pltpu.get_barrier_semaphore()
+
+    def greet(i, c):
+        pl.semaphore_signal(barrier, inc=1, device_id={"ctx": lax.rem(me + i, owners)}, device_id_type=MESH)
+        return c
+
+    lax.fori_loop(1, owners, greet, 0)
+    for i in range(1, peers):
+        pl.semaphore_signal(barrier, inc=1, device_id={"head": lax.rem(my_head + i, peers)}, device_id_type=MESH)
+    pl.semaphore_wait(barrier, owners - 1 + peers - 1)
+
+    id_copies = []
+    for i in range(1, peers):
+        peer = lax.rem(my_head + i, peers)
+        copy = pltpu.make_async_remote_copy(
+            src_ref=ids_ref.at[peer], dst_ref=idr.at[i - 1],
+            send_sem=id_sem.at[0, i - 1], recv_sem=id_sem.at[1, i - 1],
+            device_id={"head": peer}, device_id_type=MESH,
+        )
+        copy.start()
+        id_copies.append(copy)
+    sub_tok = lax.broadcasted_iota(jnp.int32, (rows, rows), 0)
+    lane_tok = lax.broadcasted_iota(jnp.int32, (rows, rows), 1)
+    eye = jnp.where(sub_tok == lane_tok, 1.0, 0.0).astype(BF16)
+    before = jnp.where(sub_tok < lane_tok, 1.0, 0.0).astype(BF16)
+    head_row = lax.broadcasted_iota(jnp.int32, (heads, rows), 0)
+    factor = jnp.zeros((heads, rows), jnp.int32)
+    for h in range(heads):
+        factor = jnp.where(head_row == h, TABLE[h % 8], factor)
+    for copy in id_copies:
+        copy.wait()
+    ids = ids_ref[my_head]
+    for i in range(1, peers):
+        ids = ids + idr[i - 1]
+    spot = (ids * factor + 29 * head_row) & (CLUSTERS - 1)
+    spot_t = nt(eye, spot.astype(F32).astype(BF16)).astype(jnp.int32)
+    for h in range(heads):
+        crow[h] = spot[h : h + 1, :]
+        ccol[h] = spot_t[:, h : h + 1]
+
+    def columns(h):
+        return pl.ds(pl.multiple_of(h * HEAD_DIM, HEAD_DIM), HEAD_DIM)
+
+    def tokens_of(h):
+        return jnp.concatenate([r[:, columns(h)] for r in (q_ref, k_ref, v_ref, g_ref)], axis=1)
+
+    def line_of(spots):
+        return (spots // each // 2) % LINE
+
+    line_row = lax.broadcasted_iota(jnp.int32, (LINE, rows), 0)
+
+    def rank(h, used):
+        row, col = crow[h], ccol[h]
+        same = col == row
+        rank_row = jnp.sum(jnp.where(same & (sub_tok < lane_tok), 1.0, 0.0), axis=0, keepdims=True)
+        rank_col = jnp.sum(jnp.where(same & (lane_tok < sub_tok), 1.0, 0.0), axis=1, keepdims=True)
+        base = (h % 2) * each
+        trow[h] = jnp.where(rank_row < 0.5, row // each * groups + base + row % each, -1)
+        tcol[h] = jnp.where(rank_col < 0.5, col // each * groups + base + col % each, -1)
+        chosen = jnp.where((line_row == line_of(row)) & (rank_row > 0.5), 1.0, 0.0)
+        ahead = nn(chosen.astype(BF16), before) + used
+        spot_in = jnp.sum(chosen * ahead, axis=0, keepdims=True)
+        spot_in = jnp.where(rank_row > 0.5, jnp.minimum(spot_in, 250.0), 250.0)
+        erow[h] = spot_in.astype(jnp.int32)
+        spot_col = nt(eye, jnp.broadcast_to(spot_in, (8, rows)).astype(BF16))[:, 0:1].astype(jnp.int32)
+        ecol[h] = jnp.where(spot_col < FIRST_CAP, line_of(col) * FIRST_CAP + spot_col, -1)
+        return used + jnp.sum(chosen, axis=1, keepdims=True)
+
+    used = lax.fori_loop(0, heads, rank, jnp.zeros((LINE, 1), F32))
+    spill = jnp.max(used, axis=0, keepdims=True) - FIRST_CAP
+
+    lane_wide = lax.broadcasted_iota(jnp.int32, (1, wide), 1)
+    key_mark = jnp.where((lane_wide >= HEAD_DIM) & (lane_wide < 2 * HEAD_DIM), 1.0, 0.0)
+
+    def build(p, c):
+        lane = jnp.concatenate([trow[2 * p], trow[2 * p + 1]], axis=1)
+        token = jnp.concatenate([tokens_of(2 * p), tokens_of(2 * p + 1)], axis=0)
+        one_hot = jnp.where(lax.broadcasted_iota(jnp.int32, (part, pair_rows), 0) == lane, 1.0, 0.0)
+        empty = jnp.where(jnp.sum(one_hot, axis=1, keepdims=True) > 0.5, 0.0, EMPTY_KEY)
+        filled = nn(one_hot.astype(BF16), token) + empty * key_mark
+        sbuf[p] = filled.astype(BF16).reshape(owners, groups, wide)
+
+        def send(i, c):
+            dst = lax.rem(me + i, owners)
+            pltpu.make_async_remote_copy(
+                src_ref=sbuf.at[p, dst], dst_ref=rbuf.at[p, me], send_sem=send_sem.at[p], recv_sem=recv_sem.at[p],
+                device_id={"ctx": dst}, device_id_type=MESH,
+            ).start()
+            return c
+
+        lax.fori_loop(1, owners, send, 0)
+        pltpu.make_async_copy(sbuf.at[p, me], rbuf.at[p, me], recv_sem.at[p]).start()
+        return c
+
+    def along_z(stage, src, dst):
+        def send(i, c):
+            z = lax.rem(my_z + i, LINE)
+            pltpu.make_async_remote_copy(
+                src_ref=src.at[z], dst_ref=dst.at[my_z], send_sem=e_send.at[stage], recv_sem=e_recv.at[stage],
+                device_id={"ctx": my_x * 16 + z * 2 + my_c}, device_id_type=MESH,
+            ).start()
+            return c
+
+        lax.fori_loop(1, LINE, send, 0)
+        pltpu.make_async_copy(src.at[my_z], dst.at[my_z], e_recv.at[stage]).start()
+
+    def across(stage, src, dst):
+        def send(i, c):
+            w = lax.rem(my_w + i, LINE)
+            pltpu.make_async_remote_copy(
+                src_ref=src.at[w], dst_ref=dst.at[my_w], send_sem=e_send.at[stage], recv_sem=e_recv.at[stage],
+                device_id={"ctx": w // 2 * 16 + my_z * 2 + w % 2}, device_id_type=MESH,
+            ).start()
+            return c
+
+        lax.fori_loop(1, LINE, send, 0)
+        pltpu.make_async_copy(src.at[my_w], dst.at[my_w], e_recv.at[stage]).start()
+
+    def arrived(stage, dst):
+        pltpu.make_async_copy(dst, dst, e_recv.at[stage]).wait()
+
+    build(0, 0)
+
+    lane_meta = lax.broadcasted_iota(jnp.int32, (rows, META), 1)
+    acc[...] = jnp.zeros_like(acc)
+
+    def second(h, c):
+        place = erow[h]
+        target = jnp.where(place < FIRST_CAP, line_of(crow[h]) * FIRST_CAP + place, -1)
+        one_hot = jnp.where(lax.broadcasted_iota(jnp.int32, (first_rows, rows), 0) == target, 1.0, 0.0).astype(BF16)
+        meta = jnp.where(lane_meta == 0, ccol[h], jnp.where(lane_meta == 1, h, jnp.where(lane_meta == 2, me, 1)))
+        meta = jnp.where(lane_meta < 4, meta, 0).astype(F32).astype(BF16)
+        acc[...] += nn(one_hot, jnp.concatenate([tokens_of(h), meta], axis=1))
+        return c
+
+    lax.fori_loop(0, heads, second, 0)
+    e1[...] = acc[...].astype(BF16).reshape(LINE, FIRST_CAP, wide + META)
+    along_z(0, e1, r1)
+
+    build(1, 0)
+    halo_copies = []
+    for i, ref in enumerate((k_ref, v_ref)):
+        copy = pltpu.make_async_remote_copy(
+            src_ref=ref, dst_ref=halo.at[i], send_sem=halo_sem.at[0, i], recv_sem=halo_sem.at[1, i],
+            device_id={"ctx": nxt}, device_id_type=MESH,
+        )
+        copy.start()
+        halo_copies.append(copy)
+    lax.fori_loop(2, pairs, build, 0)
+
+    arrived(0, r1)
+    pick = jnp.where(
+        lax.broadcasted_iota(jnp.int32, (8, META), 0) == lax.broadcasted_iota(jnp.int32, (8, META), 1), 1.0, 0.0
+    ).astype(BF16)
+    came = r1[...].reshape(first_rows, wide + META)
+    labels = nt(pick, came[:, wide:])
+    owner = labels[0:1].astype(jnp.int32) // each
+    live = labels[3:4] > 0.5
+    across_row = lax.broadcasted_iota(jnp.int32, (LINE, first_rows), 0)
+    chosen = jnp.where((across_row == owner // 16 * 2 + owner % 2) & live, 1.0, 0.0)
+    earlier = jnp.where(
+        lax.broadcasted_iota(jnp.int32, (first_rows, first_rows), 0)
+        < lax.broadcasted_iota(jnp.int32, (first_rows, first_rows), 1), 1.0, 0.0,
+    ).astype(BF16)
+    place = jnp.sum(chosen * nn(chosen.astype(BF16), earlier), axis=0, keepdims=True).astype(jnp.int32)
+    target = jnp.where(live & (place < NEXT_CAP), (owner // 16 * 2 + owner % 2) * NEXT_CAP + place, -1)
+    relay_row[...] = target
+    count = jnp.max(jnp.sum(chosen, axis=1, keepdims=True), axis=0, keepdims=True)
+    spill = jnp.maximum(spill, count - NEXT_CAP)
+    flag_out[0] = jnp.broadcast_to(jnp.where(spill > 0.5, 1.0, 0.0), (1, META))
+
+    def relay_hot():
+        hit = lax.broadcasted_iota(jnp.int32, (next_rows, first_rows), 0) == relay_row[...]
+        return jnp.where(hit, 1.0, 0.0).astype(BF16)
+
+    e2[...] = nn(relay_hot(), came).astype(BF16).reshape(LINE, NEXT_CAP, wide + META)
+    across(1, e2, r2)
+
+    for copy in halo_copies:
+        copy.wait()
+    q_pos = lax.broadcasted_iota(jnp.int32, (rows, WINDOW + rows), 0)
+    k_pos = lax.broadcasted_iota(jnp.int32, (rows, WINDOW + rows), 1) - WINDOW
+    in_window = (k_pos <= q_pos) & (k_pos > q_pos - WINDOW) & (k_pos + me * rows >= 0)
+
+    def window(h, c):
+        cols = columns(h)
+        key_all = jnp.concatenate([halo[0, :, cols], k_ref[:, cols]], axis=0)
+        value_all = jnp.concatenate([halo[1, :, cols], v_ref[:, cols]], axis=0)
+        att, gq, gk, gv = attend(q_ref[:, cols], key_all, value_all, g_ref[:, cols], in_window)
+        win[0, :, cols] = att
+        win[1, :, cols] = gq
+        win[2, :, cols] = gk[WINDOW:]
+        win[3, :, cols] = gv[WINDOW:]
+        hsend[0, :, cols] = gk[:WINDOW].astype(BF16)
+        hsend[1, :, cols] = gv[:WINDOW].astype(BF16)
+        return c
+
+    lax.fori_loop(0, heads, window, 0)
+    back_copies = []
+    for i in range(2):
+        copy = pltpu.make_async_remote_copy(
+            src_ref=hsend.at[i], dst_ref=hrecv.at[i], send_sem=hback_sem.at[0, i], recv_sem=hback_sem.at[1, i],
+            device_id={"ctx": prv}, device_id_type=MESH,
+        )
+        copy.start()
+        back_copies.append(copy)
+
+    flag_copies = []
+    for i in range(1, peers):
+        copy = pltpu.make_async_remote_copy(
+            src_ref=flag_out.at[0], dst_ref=flag_y.at[i - 1], send_sem=fy_sem.at[0, i - 1],
+            recv_sem=fy_sem.at[1, i - 1], device_id={"head": lax.rem(my_head + i, peers)}, device_id_type=MESH,
+        )
+        copy.start()
+        flag_copies.append(copy)
+    for copy in flag_copies:
+        copy.wait()
+    raised = flag_out[0]
+    for i in range(1, peers):
+        raised = jnp.maximum(raised, flag_y[i - 1])
+    flag_out[1] = raised
+
+    arrived(1, r2)
+    guests = r2[...].reshape(next_rows, wide + META)
+    labels = nt(pick, guests[:, wide:]).astype(jnp.int32)
+    spots, whose, block, live = labels[0:1], labels[1:2], labels[2:3], labels[3:4]
+    for p in range(pairs):
+        seat = ((whose % 2) * each + spots % each) * owners + block
+        expand_row[p] = jnp.where((live > 0) & (whose // 2 == p), seat, -1)
+    p_row = lax.broadcasted_iota(jnp.int32, (part, part), 0)
+    p_col = lax.broadcasted_iota(jnp.int32, (part, part), 1)
+    to_group = jnp.where(p_col == (p_row % owners) * groups + p_row // owners, 1.0, 0.0).astype(BF16)
+    from_group = jnp.where(p_col == (p_row % groups) * owners + p_row // groups, 1.0, 0.0).astype(BF16)
+    capacity = owners * SLOTS
+    a_pos = lax.broadcasted_iota(jnp.int32, (capacity, capacity), 0)
+    b_pos = lax.broadcasted_iota(jnp.int32, (capacity, capacity), 1)
+    causal = (b_pos % owners) * SLOTS + b_pos // owners <= (a_pos % owners) * SLOTS + a_pos // owners
+    first = jnp.where(lax.broadcasted_iota(jnp.int32, (8, HEAD_DIM), 1) == 0, 1.0, 0.0).astype(BF16)
+    back_acc[...] = jnp.zeros_like(back_acc)
+
+    def cluster(p, c):
+        pltpu.make_async_copy(rbuf.at[p], rbuf.at[p], recv_sem.at[p]).wait()
+        hit = lax.broadcasted_iota(jnp.int32, (part, next_rows), 0) == expand_row[p]
+        seats = jnp.where(hit, 1.0, 0.0)
+        empty = jnp.where(jnp.sum(seats, axis=1, keepdims=True) > 0.5, 0.0, EMPTY_KEY)
+        seats = seats.astype(BF16)
+        guest = r2[...].reshape(next_rows, wide + META)[:, :wide]
+        slots = [
+            nn(to_group, rbuf[p].reshape(part, wide)).astype(BF16),
+            (nn(seats, guest) + empty * key_mark).astype(BF16),
+        ]
+        results = [[], []]
+        for g in range(groups):
+            packed = jnp.concatenate([s[g * owners : (g + 1) * owners] for s in slots], axis=0)
+            query, key, value, grad = (packed[:, i * HEAD_DIM : (i + 1) * HEAD_DIM] for i in range(4))
+            valid = nt(first, key)[0:1, :] < EMPTY_KEY / 2
+            done = attend(query, key, value, grad, causal & valid)
+            done = jnp.concatenate([d.astype(BF16) for d in done], axis=1)
+            for r in range(SLOTS):
+                results[r].append(done[r * owners : (r + 1) * owners])
+        back = nn(from_group, jnp.concatenate(results[0], axis=0)).astype(BF16)
+        bsend[p] = back.reshape(owners, groups, wide)
+
+        def send(i, c):
+            dst = lax.rem(me + i, owners)
+            pltpu.make_async_remote_copy(
+                src_ref=bsend.at[p, dst], dst_ref=brecv.at[p, me], send_sem=bsend_sem.at[p],
+                recv_sem=brecv_sem.at[p], device_id={"ctx": dst}, device_id_type=MESH,
+            ).start()
+            return c
+
+        lax.fori_loop(1, owners, send, 0)
+        pltpu.make_async_copy(bsend.at[p, me], brecv.at[p, me], brecv_sem.at[p]).start()
+        back_acc[...] += tn(seats, jnp.concatenate(results[1], axis=0))
+        return c
+
+    lax.fori_loop(0, pairs, cluster, 0)
+    e3[...] = back_acc[...].astype(BF16).reshape(LINE, NEXT_CAP, wide)
+    across(2, e3, r3)
+
+    def tell(i, c):
+        dst = lax.rem(me + i, owners)
+        pltpu.make_async_remote_copy(
+            src_ref=flag_out.at[1], dst_ref=flag_in.at[me], send_sem=f_send, recv_sem=f_recv,
+            device_id={"ctx": dst}, device_id_type=MESH,
+        ).start()
+        return c
+
+    lax.fori_loop(1, owners, tell, 0)
+    pltpu.make_async_copy(flag_out.at[1], flag_in.at[me], f_recv).start()
+
+    arrived(2, r3)
+    e4[...] = tn(relay_hot(), r3[...].reshape(next_rows, wide)).astype(BF16).reshape(LINE, FIRST_CAP, wide)
+    along_z(3, e4, r4)
+
+    for copy in back_copies:
+        copy.wait()
+
+    def settle(p, c):
+        pltpu.make_async_copy(brecv.at[p], brecv.at[p], brecv_sem.at[p]).wait()
+        target = jnp.concatenate([tcol[2 * p], tcol[2 * p + 1]], axis=0)
+        hit = lax.broadcasted_iota(jnp.int32, (pair_rows, part), 1) == target
+        mine = nn(jnp.where(hit, 1.0, 0.0).astype(BF16), brecv[p].reshape(part, wide))
+        for hh in range(2):
+            cols = columns(2 * p + hh)
+            for i in range(4):
+                both = win[i, :, cols] + mine[hh * rows : (hh + 1) * rows, i * HEAD_DIM : (i + 1) * HEAD_DIM]
+                if i >= 2:
+                    both = both + hrecv[i - 2, :, cols].astype(F32)
+                win[i, :, cols] = both
+        return c
+
+    lax.fori_loop(0, pairs, settle, 0)
+    arrived(3, r4)
+
+    def finish(h, c):
+        hit = lax.broadcasted_iota(jnp.int32, (rows, first_rows), 1) == ecol[h]
+        mine = nn(jnp.where(hit, 1.0, 0.0).astype(BF16), r4[...].reshape(first_rows, wide))
+        cols = columns(h)
+        for i, out in enumerate((out_o, out_q, out_k, out_v)):
+            out[:, cols] = (win[i, :, cols] + mine[:, i * HEAD_DIM : (i + 1) * HEAD_DIM]).astype(BF16)
+        return c
+
+    lax.fori_loop(0, heads, finish, 0)
+    pltpu.make_async_copy(flag_in, flag_in, f_recv).wait()
+    out_flag[...] = jnp.max(flag_in[...], axis=0)
+
+    def drain(p, c):
+        some = pl.ds(0, owners - 1)
+        pltpu.make_async_copy(sbuf.at[p, some], sbuf.at[p, some], send_sem.at[p]).wait()
+        pltpu.make_async_copy(bsend.at[p, some], bsend.at[p, some], bsend_sem.at[p]).wait()
+        return c
+
+    lax.fori_loop(0, pairs, drain, 0)
+    some = pl.ds(0, LINE - 1)
+    for stage, ref in enumerate((e1, e2, e3, e4)):
+        pltpu.make_async_copy(ref.at[some], ref.at[some], e_send.at[stage]).wait()
+    some = pl.ds(0, owners - 1)
+    pltpu.make_async_copy(flag_in.at[some], flag_in.at[some], f_send).wait()
+
+
 def on_device(queries, keys, values, grad_out, cluster_ids):
     rows, width = queries.shape
     heads = width // HEAD_DIM
@@ -263,31 +633,52 @@
     spread = jnp.zeros((peers, heads, rows), jnp.int32)
     spread = lax.dynamic_update_slice_in_dim(spread, ids, lax.axis_index("head") * share, axis=2)
     pairs = heads // 2
-    buffer = pltpu.VMEM((pairs, owners, SLOTS, 2 * each, 4 * HEAD_DIM), BF16)
     vmem = pl.BlockSpec(memory_space=pltpu.VMEM)
     dma = pltpu.SemaphoreType.DMA
-    return pl.pallas_call(
-        functools.partial(kernel, owners, peers, heads, rows),
-        out_shape=[jax.ShapeDtypeStruct((rows, width), BF16)] * 4,
-        in_specs=[vmem] * 5,
-        out_specs=[vmem] * 4,
-        scratch_shapes=[
-            buffer, buffer, buffer, buffer,
-            pltpu.VMEM((2, WINDOW, width), BF16),
-            pltpu.VMEM((2, WINDOW, width), BF16),
-            pltpu.VMEM((2, WINDOW, width), BF16),
-            pltpu.VMEM((4, rows, width), F32),
-            pltpu.VMEM((peers - 1, heads, rows), jnp.int32),
-            pltpu.VMEM((heads, 1, rows), jnp.int32),
-            pltpu.VMEM((heads, rows, 1), jnp.int32),
-            pltpu.VMEM((heads, rows, 1), jnp.int32),
-            dma((2, peers - 1)), dma((2, 2)), dma((2, 2)),
-            dma((pairs,)), dma((pairs,)), dma((pairs,)), dma((pairs,)),
-        ],
-        compiler_params=pltpu.CompilerParams(
-            collective_id=0, has_side_effects=True, vmem_limit_bytes=60 * 1024 * 1024
-        ),
-    )(queries, keys, values, grad_out, spread)
+    args = (queries, keys, values, grad_out, spread)
+    result = jax.ShapeDtypeStruct((rows, width), BF16)
+    wide = 4 * HEAD_DIM
+
+    def call(body, outs, scratch, number):
+        return pl.pallas_call(
+            functools.partial(body, owners, peers, heads, rows),
+            out_shape=outs,
+            in_specs=[vmem] * 5,
+            out_specs=[vmem] * len(outs),
+            scratch_shapes=scratch,
+            compiler_params=pltpu.CompilerParams(
+                collective_id=number, has_side_effects=True, vmem_limit_bytes=60 * 1024 * 1024
+            ),
+        )(*args)
+
+    buffer = pltpu.VMEM((pairs, owners, SLOTS, 2 * each, wide), BF16)
+    narrow = pltpu.VMEM((pairs, owners, 2 * each, wide), BF16)
+    window = [pltpu.VMEM((2, WINDOW, width), BF16)] * 3 + [pltpu.VMEM((4, rows, width), F32)]
+    row_list = pltpu.VMEM((heads, 1, rows), jnp.int32)
+    col_list = pltpu.VMEM((heads, rows, 1), jnp.int32)
+    ids_in = pltpu.VMEM((peers - 1, heads, rows), jnp.int32)
+    sems = [dma((2, peers - 1)), dma((2, 2)), dma((2, 2)), dma((pairs,)), dma((pairs,)), dma((pairs,)), dma((pairs,))]
+
+    def line(cap, size):
+        return pltpu.VMEM((LINE, cap, size), BF16)
+
+    *outs, flag = call(
+        kernel,
+        [result] * 4 + [jax.ShapeDtypeStruct((1, META), F32)],
+        [narrow] * 4 + window + [ids_in, row_list, col_list, row_list, col_list, row_list, col_list]
+        + [pltpu.VMEM((LINE * FIRST_CAP, wide + META), F32)]
+        + [line(FIRST_CAP, wide + META)] * 2 + [line(NEXT_CAP, wide + META)] * 2
+        + [pltpu.VMEM((LINE * NEXT_CAP, wide), F32)] + [line(NEXT_CAP, wide)] * 2 + [line(FIRST_CAP, wide)] * 2
+        + [pltpu.VMEM((1, LINE * FIRST_CAP), jnp.int32), pltpu.VMEM((pairs, 1, LINE * NEXT_CAP), jnp.int32)]
+        + [pltpu.VMEM((2, 1, META), F32), pltpu.VMEM((peers - 1, 1, META), F32), pltpu.VMEM((owners, 1, META), F32)]
+        + sems + [dma((4,)), dma((4,)), dma((2, peers - 1)), dma, dma],
+        0,
+    )
+
+    def again():
+        return tuple(call(wide_kernel, [result] * 4, [buffer] * 4 + window + [ids_in, row_list, col_list, col_list] + sems, 1))
+
+    return lax.cond(flag[0, 0] > 0.5, again, lambda: tuple(outs))
 
 
 def solution(mesh):

time: 221 us -> 165 us (0.75); the launches traced: 221 us -> 163 us
  Pallas kernels: 214 us -> 157 us
    pallas_call x1, Pallas kernels: 214 us -> 157 us  [call(): pl.pallas_call(functools.partial(body, owners, peers, heads, rows), out_s...]
    unnamed x14 -> x18, local copies, waits for them, and re-layouts: 6.49 us -> 4.94 us
where the time goes in v1:
time: 165 us; the launch traced here: 163 us
  Pallas kernels  157 us (95%)
  local copies, waits for them, and re-layouts  5.06 us (3%)
    pallas_call x1, Pallas kernels, call(): pl.pallas_call(functools.partial(body, owners, peers, heads, rows), out_s...  157 us
    unnamed x18, local copies, waits for them, and re-layouts  4.94 us

profile of v1, /device:TPU:1, one launch (start us, length us, event | category | flops | bytes accessed | tf_op | source)
XLA Modules:
  0.0 162.6 jit_solution(2782515914783299605)
XLA Ops:
  0.6 0.0 copy-start.5
  0.7 0.7 copy-done.5
  1.4 0.1 dynamic_update_slice.3.ids_ref
  1.5 0.0 copy-start
  1.5 0.0 copy-start.1
  1.5 0.0 copy-start.2
  1.5 0.0 copy-start.3
  1.5 156.5 %shard_map.92 = (bf16[256,1024]{1,0:T(8,128)(2,1)S(1)}, bf16[256,1024]{1,0:T(8,128)(2,1)S(1)}, bf16[256,1024]{1,0:T(8,128)(2,1)S(1)}, bf16[256,1024]{1,0:T(8,128)(2,1)}, f32[1,128]{1,0:T(1,128)}) custom-call(bf16[256,1024]{1,0:T(8,128)(2,1)} %q_ref.1, bf16[256,1024]{1,0:T(8,128)(2,1)} %k_ref.1, bf16[256,1024]{1,0:T(8,128)(2,1)} %v_ref.1, ...), custom_call_target="tpu_custom_call" | custom-call | tf_op jit(solution)/shard_map/pallas_call | solution.py:643
  158.1 0.0 copy-start.6
  158.1 0.6 copy-done.6
  158.7 0.0 copy-done
  158.7 0.0 copy-done.1
  158.7 0.0 copy-done.2
  158.7 0.0 copy-done.3
  158.8 0.2 conditional.1
  158.9 0.8 copy.30
  159.7 0.8 copy.31
  160.5 0.0 copy-start.4
  160.5 0.8 copy.32
  161.3 0.4 copy-done.4
  161.8 0.8 copy.33
  (1 shorter events, 0.0 us)
Async XLA Ops:
  0.6 0.7 copy-start.5
  1.5 157.2 %copy-start = (bf16[256,1024]{1,0:T(8,128)(2,1)S(1)}, bf16[256,1024]{1,0:T(8,128)(2,1)}, u32[]{:S(2)}) copy-start(bf16[256,1024]{1,0:T(8,128)(2,1)} %q_ref.1) | copy-start | bytes 1572868
  1.5 157.2 %copy-start.1 = (bf16[256,1024]{1,0:T(8,128)(2,1)S(1)}, bf16[256,1024]{1,0:T(8,128)(2,1)}, u32[]{:S(2)}) copy-start(bf16[256,1024]{1,0:T(8,128)(2,1)} %k_ref.1) | copy-start | bytes 1572868
  1.5 157.2 %copy-start.2 = (bf16[256,1024]{1,0:T(8,128)(2,1)S(1)}, bf16[256,1024]{1,0:T(8,128)(2,1)}, u32[]{:S(2)}) copy-start(bf16[256,1024]{1,0:T(8,128)(2,1)} %v_ref.1) | copy-start | bytes 1572868
  1.5 157.2 %copy-start.3 = (bf16[256,1024]{1,0:T(8,128)(2,1)S(1)}, bf16[256,1024]{1,0:T(8,128)(2,1)}, u32[]{:S(2)}) copy-start(bf16[256,1024]{1,0:T(8,128)(2,1)} %g_ref.1) | copy-start | bytes 1572868
  158.1 0.6 copy-start.6
  160.5 1.2 copy-start.4

commit v2 on v1

--- a/solution.py
+++ b/solution.py
@@ -45,6 +45,35 @@
     grad_key = tn(grad_scores, query) * SCALE
     grad_value = tn(weights16, grad)
     return attended, grad_query, grad_key, grad_value
+
+
+def attend_groups(packed, allowed):
+    size = packed[0].shape[0]
+    query, key, value, grad = (
+        [one[:, i * HEAD_DIM : (i + 1) * HEAD_DIM] for one in packed] for i in range(4)
+    )
+
+    def each(product, left, right):
+        return jnp.concatenate([product(a, b) for a, b in zip(left, right)], axis=0)
+
+    def split(rows):
+        return [rows[i * size : (i + 1) * size] for i in range(len(packed))]
+
+    scores = jnp.where(allowed, each(nt, query, key) * SCALE, NEG_LARGE)
+    top = jnp.max(scores, axis=-1, keepdims=True)
+    exps = jnp.where(allowed, jnp.exp(scores - top), 0.0)
+    total = jnp.maximum(jnp.sum(exps, axis=-1, keepdims=True), 1.0)
+    weights16 = (exps * (1.0 / total)).astype(BF16)
+    parts = split(weights16)
+    attended = each(nn, parts, value)
+    row_dot = jnp.sum(jnp.concatenate(grad, axis=0).astype(F32) * attended, axis=-1, keepdims=True)
+    grad_scores = (weights16.astype(F32) * (each(nt, grad, value) - row_dot)).astype(BF16)
+    changes = split(grad_scores)
+    grad_query = each(nn, changes, key) * SCALE
+    grad_key = each(tn, changes, query) * SCALE
+    grad_value = each(tn, parts, grad)
+    done = jnp.concatenate([d.astype(BF16) for d in (attended, grad_query, grad_key, grad_value)], axis=1)
+    return split(done)
 
 
 def wide_kernel(
@@ -254,18 +283,19 @@
 
 TABLE = (1, 37, 91, 151, 203, 117, 173, 55)
 LINE = 8
-FIRST_CAP = 48
+FIRST_CAP = 40
 NEXT_CAP = 80
 META = 128
 
 
 def kernel(
     owners, peers, heads, rows,
-    q_ref, k_ref, v_ref, g_ref, ids_ref,
+    q_hbm, k_hbm, v_hbm, g_hbm, ids_ref,
     out_o, out_q, out_k, out_v, out_flag,
-    sbuf, rbuf, bsend, brecv, halo, hsend, hrecv, win, idr, crow, ccol, trow, tcol, erow, ecol,
-    acc, e1, r1, e2, r2, back_acc, e3, r3, e4, r4, relay_row, expand_row, flag_out, flag_y, flag_in,
-    id_sem, halo_sem, hback_sem, send_sem, recv_sem, bsend_sem, brecv_sem, e_send, e_recv, fy_sem, f_send, f_recv,
+    q_ref, k_ref, v_ref, g_ref, win, r4, ecol,
+    sbuf, rbuf, bsend, brecv, halo, hsend, hrecv, idr, crow, ccol, trow, tcol, erow,
+    acc, e1, r1, e2, r2, back_acc, e3, r3, e4, relay_row, expand_row, flag_out, flag_y, flag_in,
+    id_sem, halo_sem, hback_sem, send_sem, recv_sem, bsend_sem, brecv_sem, e_send, e_recv, fy_sem, f_send, f_recv, in_sem,
 ):
     me = lax.axis_index("ctx")
     my_head = lax.axis_index("head")
@@ -281,13 +311,20 @@
     wide = 4 * HEAD_DIM
     first_rows, next_rows = LINE * FIRST_CAP, LINE * NEXT_CAP
 
+    loads = [
+        pltpu.make_async_copy(src, dst, in_sem.at[i])
+        for i, (src, dst) in enumerate(((k_hbm, k_ref), (v_hbm, v_ref), (q_hbm, q_ref), (g_hbm, g_ref)))
+    ]
+    for load in loads:
+        load.start()
     barrier = pltpu.get_barrier_semaphore()
 
     def greet(i, c):
-        pl.semaphore_signal(barrier, inc=1, device_id={"ctx": lax.rem(me + i, owners)}, device_id_type=MESH)
-        return c
-
-    lax.fori_loop(1, owners, greet, 0)
+        far = lax.rem(i + owners // 2 + 7, owners - 1) + 1
+        pl.semaphore_signal(barrier, inc=1, device_id={"ctx": lax.rem(me + far, owners)}, device_id_type=MESH)
+        return c
+
+    lax.fori_loop(0, owners - 1, greet, 0)
     for i in range(1, peers):
         pl.semaphore_signal(barrier, inc=1, device_id={"head": lax.rem(my_head + i, peers)}, device_id_type=MESH)
     pl.semaphore_wait(barrier, owners - 1 + peers - 1)
@@ -302,6 +339,16 @@
         )
         copy.start()
         id_copies.append(copy)
+    for load in loads:
+        load.wait()
+    halo_copies = []
+    for i, ref in enumerate((k_ref, v_ref)):
+        copy = pltpu.make_async_remote_copy(
+            src_ref=ref, dst_ref=halo.at[i], send_sem=halo_sem.at[0, i], recv_sem=halo_sem.at[1, i],
+            device_id={"ctx": nxt}, device_id_type=MESH,
+        )
+        copy.start()
+        halo_copies.append(copy)
     sub_tok = lax.broadcasted_iota(jnp.int32, (rows, rows), 0)
     lane_tok = lax.broadcasted_iota(jnp.int32, (rows, rows), 1)
     eye = jnp.where(sub_tok == lane_tok, 1.0, 0.0).astype(BF16)
@@ -349,8 +396,7 @@
         ecol[h] = jnp.where(spot_col < FIRST_CAP, line_of(col) * FIRST_CAP + spot_col, -1)
         return used + jnp.sum(chosen, axis=1, keepdims=True)
 
-    used = lax.fori_loop(0, heads, rank, jnp.zeros((LINE, 1), F32))
-    spill = jnp.max(used, axis=0, keepdims=True) - FIRST_CAP
+    used = lax.fori_loop(0, 2, rank, jnp.zeros((LINE, 1), F32))
 
     lane_wide = lax.broadcasted_iota(jnp.int32, (1, wide), 1)
     key_mark = jnp.where((lane_wide >= HEAD_DIM) & (lane_wide < 2 * HEAD_DIM), 1.0, 0.0)
@@ -403,6 +449,8 @@
         pltpu.make_async_copy(dst, dst, e_recv.at[stage]).wait()
 
     build(0, 0)
+    used = lax.fori_loop(2, heads, rank, used)
+    spill = jnp.max(used, axis=0, keepdims=True) - FIRST_CAP
 
     lane_meta = lax.broadcasted_iota(jnp.int32, (rows, META), 1)
     acc[...] = jnp.zeros_like(acc)
@@ -421,15 +469,37 @@
     along_z(0, e1, r1)
 
     build(1, 0)
-    halo_copies = []
-    for i, ref in enumerate((k_ref, v_ref)):
+
+    for copy in halo_copies:
+        copy.wait()
+    q_pos = lax.broadcasted_iota(jnp.int32, (rows, WINDOW + rows), 0)
+    k_pos = lax.broadcasted_iota(jnp.int32, (rows, WINDOW + rows), 1) - WINDOW
+    in_window = (k_pos <= q_pos) & (k_pos > q_pos - WINDOW) & (k_pos + me * rows >= 0)
+
+    def window(h, c):
+        cols = columns(h)
+        key_all = jnp.concatenate([halo[0, :, cols], k_ref[:, cols]], axis=0)
+        value_all = jnp.concatenate([halo[1, :, cols], v_ref[:, cols]], axis=0)
+        att, gq, gk, gv = attend(q_ref[:, cols], key_all, value_all, g_ref[:, cols], in_window)
+        win[0, :, cols] = att
+        win[1, :, cols] = gq
+        win[2, :, cols] = gk[WINDOW:]
+        win[3, :, cols] = gv[WINDOW:]
+        hsend[0, :, cols] = gk[:WINDOW].astype(BF16)
+        hsend[1, :, cols] = gv[:WINDOW].astype(BF16)
+        return c
+
+    lax.fori_loop(0, heads, window, 0)
+    back_copies = []
+    for i in range(2):
         copy = pltpu.make_async_remote_copy(
-            src_ref=ref, dst_ref=halo.at[i], send_sem=halo_sem.at[0, i], recv_sem=halo_sem.at[1, i],
-            device_id={"ctx": nxt}, device_id_type=MESH,
+            src_ref=hsend.at[i], dst_ref=hrecv.at[i], send_sem=hback_sem.at[0, i], recv_sem=hback_sem.at[1, i],
+            device_id={"ctx": prv}, device_id_type=MESH,
         )
         copy.start()
-        halo_copies.append(copy)
-    lax.fori_loop(2, pairs, build, 0)
+        back_copies.append(copy)
+
+    lax.fori_loop(2, pairs - 1, build, 0)
 
     arrived(0, r1)
     pick = jnp.where(
@@ -459,35 +529,6 @@
     e2[...] = nn(relay_hot(), came).astype(BF16).reshape(LINE, NEXT_CAP, wide + META)
     across(1, e2, r2)
 
-    for copy in halo_copies:
-        copy.wait()
-    q_pos = lax.broadcasted_iota(jnp.int32, (rows, WINDOW + rows), 0)
-    k_pos = lax.broadcasted_iota(jnp.int32, (rows, WINDOW + rows), 1) - WINDOW
-    in_window = (k_pos <= q_pos) & (k_pos > q_pos - WINDOW) & (k_pos + me * rows >= 0)
-
-    def window(h, c):
-        cols = columns(h)
-        key_all = jnp.concatenate([halo[0, :, cols], k_ref[:, cols]], axis=0)
-        value_all = jnp.concatenate([halo[1, :, cols], v_ref[:, cols]], axis=0)
-        att, gq, gk, gv = attend(q_ref[:, cols], key_all, value_all, g_ref[:, cols], in_window)
-        win[0, :, cols] = att
-        win[1, :, cols] = gq
-        win[2, :, cols] = gk[WINDOW:]
-        win[3, :, cols] = gv[WINDOW:]
-        hsend[0, :, cols] = gk[:WINDOW].astype(BF16)
-        hsend[1, :, cols] = gv[:WINDOW].astype(BF16)
-        return c
-
-    lax.fori_loop(0, heads, window, 0)
-    back_copies = []
-    for i in range(2):
-        copy = pltpu.make_async_remote_copy(
-            src_ref=hsend.at[i], dst_ref=hrecv.at[i], send_sem=hback_sem.at[0, i], recv_sem=hback_sem.at[1, i],
-            device_id={"ctx": prv}, device_id_type=MESH,
-        )
-        copy.start()
-        back_copies.append(copy)
-
     flag_copies = []
     for i in range(1, peers):
         copy = pltpu.make_async_remote_copy(
@@ -496,12 +537,7 @@
         )
         copy.start()
         flag_copies.append(copy)
-    for copy in flag_copies:
-        copy.wait()
-    raised = flag_out[0]
-    for i in range(1, peers):
-        raised = jnp.maximum(raised, flag_y[i - 1])
-    flag_out[1] = raised
+    build(pairs - 1, 0)
 
     arrived(1, r2)
     guests = r2[...].reshape(next_rows, wide + META)
@@ -521,6 +557,18 @@
     first = jnp.where(lax.broadcasted_iota(jnp.int32, (8, HEAD_DIM), 1) == 0, 1.0, 0.0).astype(BF16)
     back_acc[...] = jnp.zeros_like(back_acc)
 
+    def give(p):
+        def send(i, c):
+            dst = lax.rem(me + i, owners)
+            pltpu.make_async_remote_copy(
+                src_ref=bsend.at[p, dst], dst_ref=brecv.at[p, me], send_sem=bsend_sem.at[p],
+                recv_sem=brecv_sem.at[p], device_id={"ctx": dst}, device_id_type=MESH,
+            ).start()
+            return c
+
+        lax.fori_loop(1, owners, send, 0)
+        pltpu.make_async_copy(bsend.at[p, me], brecv.at[p, me], brecv_sem.at[p]).start()
+
     def cluster(p, c):
         pltpu.make_async_copy(rbuf.at[p], rbuf.at[p], recv_sem.at[p]).wait()
         hit = lax.broadcasted_iota(jnp.int32, (part, next_rows), 0) == expand_row[p]
@@ -532,34 +580,30 @@
             nn(to_group, rbuf[p].reshape(part, wide)).astype(BF16),
             (nn(seats, guest) + empty * key_mark).astype(BF16),
         ]
-        results = [[], []]
-        for g in range(groups):
-            packed = jnp.concatenate([s[g * owners : (g + 1) * owners] for s in slots], axis=0)
-            query, key, value, grad = (packed[:, i * HEAD_DIM : (i + 1) * HEAD_DIM] for i in range(4))
-            valid = nt(first, key)[0:1, :] < EMPTY_KEY / 2
-            done = attend(query, key, value, grad, causal & valid)
-            done = jnp.concatenate([d.astype(BF16) for d in done], axis=1)
-            for r in range(SLOTS):
-                results[r].append(done[r * owners : (r + 1) * owners])
+        packed = [
+            jnp.concatenate([one[g * owners : (g + 1) * owners] for one in slots], axis=0) for g in range(groups)
+        ]
+        allowed = jnp.concatenate(
+            [causal & (nt(first, one[:, HEAD_DIM : 2 * HEAD_DIM])[0:1, :] < EMPTY_KEY / 2) for one in packed], axis=0
+        )
+        done = attend_groups(packed, allowed)
+        results = [[one[r * owners : (r + 1) * owners] for one in done] for r in range(SLOTS)]
         back = nn(from_group, jnp.concatenate(results[0], axis=0)).astype(BF16)
         bsend[p] = back.reshape(owners, groups, wide)
-
-        def send(i, c):
-            dst = lax.rem(me + i, owners)
-            pltpu.make_async_remote_copy(
-                src_ref=bsend.at[p, dst], dst_ref=brecv.at[p, me], send_sem=bsend_sem.at[p],
-                recv_sem=brecv_sem.at[p], device_id={"ctx": dst}, device_id_type=MESH,
-            ).start()
-            return c
-
-        lax.fori_loop(1, owners, send, 0)
-        pltpu.make_async_copy(bsend.at[p, me], brecv.at[p, me], brecv_sem.at[p]).start()
+        pl.when(p < pairs - 1)(lambda: give(p))
+
         back_acc[...] += tn(seats, jnp.concatenate(results[1], axis=0))
         return c
 
     lax.fori_loop(0, pairs, cluster, 0)
     e3[...] = back_acc[...].astype(BF16).reshape(LINE, NEXT_CAP, wide)
     across(2, e3, r3)
+    for copy in flag_copies:
+        copy.wait()
+    raised = flag_out[0]
+    for i in range(1, peers):
+        raised = jnp.maximum(raised, flag_y[i - 1])
+    flag_out[1] = raised
 
     def tell(i, c):
         dst = lax.rem(me + i, owners)
@@ -575,11 +619,14 @@
     arrived(2, r3)
     e4[...] = tn(relay_hot(), r3[...].reshape(next_rows, wide)).astype(BF16).reshape(LINE, FIRST_CAP, wide)
     along_z(3, e4, r4)
+    give(pairs - 1)
 
     for copy in back_copies:
         copy.wait()
 
-    def settle(p, c):
+    outs = (out_o, out_q, out_k, out_v)
+
+    def settle(p):
         pltpu.make_async_copy(brecv.at[p], brecv.at[p], brecv_sem.at[p]).wait()
         target = jnp.concatenate([tcol[2 * p], tcol[2 * p + 1]], axis=0)
         hit = lax.broadcasted_iota(jnp.int32, (pair_rows, part), 1) == target
@@ -588,23 +635,35 @@
             cols = columns(2 * p + hh)
             for i in range(4):
                 both = win[i, :, cols] + mine[hh * rows : (hh + 1) * rows, i * HEAD_DIM : (i + 1) * HEAD_DIM]
-                if i >= 2:
-                    both = both + hrecv[i - 2, :, cols].astype(F32)
-                win[i, :, cols] = both
-        return c
-
-    lax.fori_loop(0, pairs, settle, 0)
+                yield i, cols, both + hrecv[i - 2, :, cols].astype(F32) if i >= 2 else both
+
+    def settle_in(p, c):
+        for i, cols, both in settle(p):
+            win[i, :, cols] = both
+        return c
+
+    lax.fori_loop(0, pairs - 1, settle_in, 0)
     arrived(3, r4)
 
-    def finish(h, c):
+    def late(h):
         hit = lax.broadcasted_iota(jnp.int32, (rows, first_rows), 1) == ecol[h]
         mine = nn(jnp.where(hit, 1.0, 0.0).astype(BF16), r4[...].reshape(first_rows, wide))
-        cols = columns(h)
-        for i, out in enumerate((out_o, out_q, out_k, out_v)):
-            out[:, cols] = (win[i, :, cols] + mine[:, i * HEAD_DIM : (i + 1) * HEAD_DIM]).astype(BF16)
-        return c
-
-    lax.fori_loop(0, heads, finish, 0)
+        return [win[i, :, columns(h)] + mine[:, i * HEAD_DIM : (i + 1) * HEAD_DIM] for i in range(4)]
+
+    def late_in(h, c):
+        for i, both in enumerate(late(h)):
+            win[i, :, columns(h)] = both
+        return c
+
+    def late_out(h, c):
+        for i, both in enumerate(late(h)):
+            outs[i][:, columns(h)] = both.astype(BF16)
+        return c
+
+    lax.fori_loop(heads - 2, heads, late_in, 0)
+    lax.fori_loop(0, heads - 2, late_out, 0)
+    for i, cols, both in settle(pairs - 1):
+        outs[i][:, cols] = both.astype(BF16)
     pltpu.make_async_copy(flag_in, flag_in, f_recv).wait()
     out_flag[...] = jnp.max(flag_in[...], axis=0)
 
@@ -620,6 +679,13 @@
         pltpu.make_async_copy(ref.at[some], ref.at[some], e_send.at[stage]).wait()
     some = pl.ds(0, owners - 1)
     pltpu.make_async_copy(flag_in.at[some], flag_in.at[some], f_send).wait()
+
+
+def finish_kernel(*refs):
+    p = pl.program_id(0)
+    for src, out in zip(refs[:4], refs[4:]):
+        size = out.shape[0]
+        out[...] = src[pl.ds(pl.multiple_of(p * size, size), size), :]
 
 
 def on_device(queries, keys, values, grad_out, cluster_ids):
@@ -639,21 +705,24 @@
     result = jax.ShapeDtypeStruct((rows, width), BF16)
     wide = 4 * HEAD_DIM
 
-    def call(body, outs, scratch, number):
+    anywhere = pl.BlockSpec(memory_space=pl.ANY)
+
+    def call(body, outs, scratch, number, ins=None, places=None):
         return pl.pallas_call(
             functools.partial(body, owners, peers, heads, rows),
             out_shape=outs,
-            in_specs=[vmem] * 5,
-            out_specs=[vmem] * len(outs),
+            in_specs=ins or [vmem] * 5,
+            out_specs=places or [vmem] * len(outs),
             scratch_shapes=scratch,
             compiler_params=pltpu.CompilerParams(
-                collective_id=number, has_side_effects=True, vmem_limit_bytes=60 * 1024 * 1024
+                collective_id=number, has_side_effects=True, vmem_limit_bytes=36 * 1024 * 1024
             ),
         )(*args)
 
     buffer = pltpu.VMEM((pairs, owners, SLOTS, 2 * each, wide), BF16)
     narrow = pltpu.VMEM((pairs, owners, 2 * each, wide), BF16)
-    window = [pltpu.VMEM((2, WINDOW, width), BF16)] * 3 + [pltpu.VMEM((4, rows, width), F32)]
+    window = [pltpu.VMEM((2, WINDOW, width), BF16)] * 3
+    total = pltpu.VMEM((4, rows, width), F32)
     row_list = pltpu.VMEM((heads, 1, rows), jnp.int32)
     col_list = pltpu.VMEM((heads, rows, 1), jnp.int32)
     ids_in = pltpu.VMEM((peers - 1, heads, rows), jnp.int32)
@@ -665,20 +734,32 @@
     *outs, flag = call(
         kernel,
         [result] * 4 + [jax.ShapeDtypeStruct((1, META), F32)],
-        [narrow] * 4 + window + [ids_in, row_list, col_list, row_list, col_list, row_list, col_list]
+        [pltpu.VMEM((rows, width), BF16)] * 4 + [total, line(FIRST_CAP, wide), col_list] + [narrow] * 4 + window + [ids_in, row_list, col_list, row_list, col_list, row_list]
         + [pltpu.VMEM((LINE * FIRST_CAP, wide + META), F32)]
         + [line(FIRST_CAP, wide + META)] * 2 + [line(NEXT_CAP, wide + META)] * 2
-        + [pltpu.VMEM((LINE * NEXT_CAP, wide), F32)] + [line(NEXT_CAP, wide)] * 2 + [line(FIRST_CAP, wide)] * 2
+        + [pltpu.VMEM((LINE * NEXT_CAP, wide), F32)] + [line(NEXT_CAP, wide)] * 2 + [line(FIRST_CAP, wide)]
         + [pltpu.VMEM((1, LINE * FIRST_CAP), jnp.int32), pltpu.VMEM((pairs, 1, LINE * NEXT_CAP), jnp.int32)]
         + [pltpu.VMEM((2, 1, META), F32), pltpu.VMEM((peers - 1, 1, META), F32), pltpu.VMEM((owners, 1, META), F32)]
-        + sems + [dma((4,)), dma((4,)), dma((2, peers - 1)), dma, dma],
+        + sems + [dma((4,)), dma((4,)), dma((2, peers - 1)), dma, dma, dma((4,))],
         0,
+        [anywhere] * 4 + [vmem],
+        [vmem] * 5,
     )
 
     def again():
-        return tuple(call(wide_kernel, [result] * 4, [buffer] * 4 + window + [ids_in, row_list, col_list, col_list] + sems, 1))
-
-    return lax.cond(flag[0, 0] > 0.5, again, lambda: tuple(outs))
+        return tuple(
+            call(wide_kernel, [result] * 4, [buffer] * 4 + window + [total, ids_in, row_list, col_list, col_list] + sems, 1)
+        )
+
+    outs = lax.cond(flag[0, 0] > 0.5, again, lambda: tuple(outs))
+    return pl.pallas_call(
+        finish_kernel,
+        grid=(pairs,),
+        out_shape=[result] * 4,
+        in_specs=[vmem] * 4,
+        out_specs=[pl.BlockSpec((rows // pairs, width), lambda p: (p, 0))] * 4,
+        compiler_params=pltpu.CompilerParams(vmem_limit_bytes=24 * 1024 * 1024),
+    )(*outs)
 
 
 def solution(mesh):

time: 165 us -> 143 us (0.87); the launches traced: 163 us -> 143 us
  Pallas kernels: 157 us -> 141 us
  local copies, waits for them, and re-layouts: 5.06 us -> 0.84 us
    pallas_call x1, Pallas kernels: 157 us -> 139 us  [call(): pl.pallas_call(functools.partial(body, owners, peers, heads, rows), out_s...]
    unnamed x18 -> x10, local copies, waits for them, and re-layouts: 4.94 us -> 0.72 us
    pallas_call x0 -> x1, Pallas kernels: none -> 1.85 us  [on_device(): pl.pallas_call(finish_kernel, grid=(pairs,), out_shape=[result] * 4, in_s...]
where the time goes in v2:
time: 143 us
  Pallas kernels  141 us (99%)
    pallas_call x1, Pallas kernels, call(): pl.pallas_call(functools.partial(body, owners, peers, heads, rows), out_s...  139 us

profile of v2, /device:TPU:1, one launch (start us, length us, event | category | flops | bytes accessed | tf_op | source)
XLA Modules:
  0.0 142.9 jit_solution(3548204153385708044)
XLA Ops:
  0.6 0.0 copy-start.4
  0.7 0.7 copy-done.4
  1.4 0.1 dynamic_update_slice.3.ids_ref
  1.5 0.0 copy-start
  1.5 0.0 copy-start.1
  1.5 0.0 copy-start.2
  1.5 0.0 copy-start.3
  1.5 139.2 %shard_map.84 = (bf16[256,1024]{1,0:T(8,128)(2,1)S(1)}, bf16[256,1024]{1,0:T(8,128)(2,1)S(1)}, bf16[256,1024]{1,0:T(8,128)(2,1)S(1)}, bf16[256,1024]{1,0:T(8,128)(2,1)S(1)}, f32[1,128]{1,0:T(1,128)S(1)}) custom-call(bf16[256,1024]{1,0:T(8,128)(2,1)} %q_hbm.1, bf16[256,1024]{1,0:T(8,128)(2,1)} %k_hbm.1, bf16[256,1024]{1,0:T(8,128)(2,1)} %v_hbm.1, ...), custom_call_target="tpu_custom_call" | custom-call | tf_op jit(solution)/shard_map/pallas_call | solution.py:711
  140.8 0.0 copy-done
  140.8 0.0 copy-done.1
  140.8 0.0 copy-done.2
  140.8 0.0 copy-done.3
  140.8 0.2 conditional.1
  141.0 1.8 %shard_map.85 = (bf16[256,1024]{1,0:T(8,128)(2,1)}, bf16[256,1024]{1,0:T(8,128)(2,1)}, bf16[256,1024]{1,0:T(8,128)(2,1)}, bf16[256,1024]{1,0:T(8,128)(2,1)}) custom-call(bf16[256,1024]{1,0:T(8,128)(2,1)S(1)} %get-tuple-element.41.refs_0_, bf16[256,1024]{1,0:T(8,128)(2,1)S(1)} %get-tuple-element.42.refs_1_, bf16[256,1024]{1,0:T(8,128)(2,1)S(1)} %get-tuple-element.43.refs_2_, ...), custom_call_target="tpu_custom_call" | custom-call | tf_op jit(solution)/shard_map/pallas_call | solution.py:755
  (1 shorter events, 0.0 us)
Async XLA Ops:
  0.6 0.7 copy-start.4
  1.5 139.3 %copy-start = (bf16[256,1024]{1,0:T(8,128)(2,1)S(1)}, bf16[256,1024]{1,0:T(8,128)(2,1)}, u32[]{:S(2)}) copy-start(bf16[256,1024]{1,0:T(8,128)(2,1)} %q_hbm.1) | copy-start | bytes 1572868
  1.5 139.3 %copy-start.1 = (bf16[256,1024]{1,0:T(8,128)(2,1)S(1)}, bf16[256,1024]{1,0:T(8,128)(2,1)}, u32[]{:S(2)}) copy-start(bf16[256,1024]{1,0:T(8,128)(2,1)} %k_hbm.1) | copy-start | bytes 1572868
  1.5 139.3 %copy-start.2 = (bf16[256,1024]{1,0:T(8,128)(2,1)S(1)}, bf16[256,1024]{1,0:T(8,128)(2,1)}, u32[]{:S(2)}) copy-start(bf16[256,1024]{1,0:T(8,128)(2,1)} %v_hbm.1) | copy-start | bytes 1572868
  1.5 139.3 %copy-start.3 = (bf16[256,1024]{1,0:T(8,128)(2,1)S(1)}, bf16[256,1024]{1,0:T(8,128)(2,1)}, u32[]{:S(2)}) copy-start(bf16[256,1024]{1,0:T(8,128)(2,1)} %g_hbm.1) | copy-start | bytes 1572868

commit v3 on v2

--- a/solution.py
+++ b/solution.py
@@ -293,9 +293,9 @@
     q_hbm, k_hbm, v_hbm, g_hbm, ids_ref,
     out_o, out_q, out_k, out_v, out_flag,
     q_ref, k_ref, v_ref, g_ref, win, r4, ecol,
-    sbuf, rbuf, bsend, brecv, halo, hsend, hrecv, idr, crow, ccol, trow, tcol, erow,
+    sbuf, rbuf, bsend, brecv, halo, stat, stat_send, stat_recv, idr, crow, ccol, trow, tcol, erow,
     acc, e1, r1, e2, r2, back_acc, e3, r3, e4, relay_row, expand_row, flag_out, flag_y, flag_in,
-    id_sem, halo_sem, hback_sem, send_sem, recv_sem, bsend_sem, brecv_sem, e_send, e_recv, fy_sem, f_send, f_recv, in_sem,
+    id_sem, halo_sem, stat_sem, send_sem, recv_sem, bsend_sem, brecv_sem, e_send, e_recv, fy_sem, f_send, f_recv, in_sem,
 ):
     me = lax.axis_index("ctx")
     my_head = lax.axis_index("head")
@@ -342,10 +342,10 @@
     for load in loads:
         load.wait()
     halo_copies = []
-    for i, ref in enumerate((k_ref, v_ref)):
+    for i, ref in enumerate((k_ref, v_ref, q_ref, g_ref)):
         copy = pltpu.make_async_remote_copy(
             src_ref=ref, dst_ref=halo.at[i], send_sem=halo_sem.at[0, i], recv_sem=halo_sem.at[1, i],
-            device_id={"ctx": nxt}, device_id_type=MESH,
+            device_id={"ctx": nxt if i < 2 else prv}, device_id_type=MESH,
         )
         copy.start()
         halo_copies.append(copy)
@@ -470,34 +470,42 @@
 
     build(1, 0)
 
-    for copy in halo_copies:
+    for copy in halo_copies[:2]:
         copy.wait()
     q_pos = lax.broadcasted_iota(jnp.int32, (rows, WINDOW + rows), 0)
     k_pos = lax.broadcasted_iota(jnp.int32, (rows, WINDOW + rows), 1) - WINDOW
     in_window = (k_pos <= q_pos) & (k_pos > q_pos - WINDOW) & (k_pos + me * rows >= 0)
+    lane_stat = lax.broadcasted_iota(jnp.int32, (rows, META), 1)
 
     def window(h, c):
         cols = columns(h)
+        query, grad = q_ref[:, cols], g_ref[:, cols]
         key_all = jnp.concatenate([halo[0, :, cols], k_ref[:, cols]], axis=0)
         value_all = jnp.concatenate([halo[1, :, cols], v_ref[:, cols]], axis=0)
-        att, gq, gk, gv = attend(q_ref[:, cols], key_all, value_all, g_ref[:, cols], in_window)
-        win[0, :, cols] = att
-        win[1, :, cols] = gq
-        win[2, :, cols] = gk[WINDOW:]
-        win[3, :, cols] = gv[WINDOW:]
-        hsend[0, :, cols] = gk[:WINDOW].astype(BF16)
-        hsend[1, :, cols] = gv[:WINDOW].astype(BF16)
-        return c
-
+        scores = jnp.where(in_window, nt(query, key_all) * SCALE, NEG_LARGE)
+        top = jnp.max(scores, axis=-1, keepdims=True)
+        exps = jnp.where(in_window, jnp.exp(scores - top), 0.0)
+        inverse = 1.0 / jnp.sum(exps, axis=-1, keepdims=True)
+        weights16 = (exps * inverse).astype(BF16)
+        attended = nn(weights16, value_all)
+        row_dot = jnp.sum(grad.astype(F32) * attended, axis=-1, keepdims=True)
+        grad_scores = (weights16.astype(F32) * (nt(grad, value_all) - row_dot)).astype(BF16)
+        win[0, :, cols] = attended
+        win[1, :, cols] = nn(grad_scores, key_all) * SCALE
+        win[2, :, cols] = tn(grad_scores[:, WINDOW:], query) * SCALE
+        win[3, :, cols] = tn(weights16[:, WINDOW:], grad)
+        old = jnp.where(lane_stat == h, top, stat[...])
+        stat[...] = jnp.where(lane_stat == heads + h, inverse, jnp.where(lane_stat == 2 * heads + h, row_dot, old))
+        return c
+
+    stat[...] = jnp.zeros_like(stat)
     lax.fori_loop(0, heads, window, 0)
-    back_copies = []
-    for i in range(2):
-        copy = pltpu.make_async_remote_copy(
-            src_ref=hsend.at[i], dst_ref=hrecv.at[i], send_sem=hback_sem.at[0, i], recv_sem=hback_sem.at[1, i],
-            device_id={"ctx": prv}, device_id_type=MESH,
-        )
-        copy.start()
-        back_copies.append(copy)
+    stat_send[...] = stat[...].T[: 4 * heads].reshape(4 * heads, 1, rows)
+    stat_copy = pltpu.make_async_remote_copy(
+        src_ref=stat_send, dst_ref=stat_recv, send_sem=stat_sem.at[0], recv_sem=stat_sem.at[1],
+        device_id={"ctx": prv}, device_id_type=MESH,
+    )
+    stat_copy.start()
 
     lax.fori_loop(2, pairs - 1, build, 0)
 
@@ -616,13 +624,29 @@
     lax.fori_loop(1, owners, tell, 0)
     pltpu.make_async_copy(flag_out.at[1], flag_in.at[me], f_recv).start()
 
+    for copy in halo_copies[2:]:
+        copy.wait()
+    stat_copy.wait()
+    seen = (sub_tok > lane_tok) & (me < owners - 1)
+
+    def ahead(h, c):
+        cols = columns(h)
+        query, grad = halo[2, :, cols], halo[3, :, cols]
+        scores = nt(k_ref[:, cols], query) * SCALE
+        exps = jnp.exp(jnp.where(seen, scores - stat_recv[h], NEG_LARGE))
+        weights16 = (exps * stat_recv[heads + h]).astype(BF16)
+        change = nt(v_ref[:, cols], grad) - stat_recv[2 * heads + h]
+        grad_scores = (weights16.astype(F32) * change).astype(BF16)
+        win[2, :, cols] += nn(grad_scores, query) * SCALE
+        win[3, :, cols] += nn(weights16, grad)
+        return c
+
+    lax.fori_loop(0, heads, ahead, 0)
     arrived(2, r3)
     e4[...] = tn(relay_hot(), r3[...].reshape(next_rows, wide)).astype(BF16).reshape(LINE, FIRST_CAP, wide)
     along_z(3, e4, r4)
     give(pairs - 1)
 
-    for copy in back_copies:
-        copy.wait()
 
     outs = (out_o, out_q, out_k, out_v)
 
@@ -635,7 +659,7 @@
             cols = columns(2 * p + hh)
             for i in range(4):
                 both = win[i, :, cols] + mine[hh * rows : (hh + 1) * rows, i * HEAD_DIM : (i + 1) * HEAD_DIM]
-                yield i, cols, both + hrecv[i - 2, :, cols].astype(F32) if i >= 2 else both
+                yield i, cols, both
 
     def settle_in(p, c):
         for i, cols, both in settle(p):
@@ -734,13 +758,16 @@
     *outs, flag = call(
         kernel,
         [result] * 4 + [jax.ShapeDtypeStruct((1, META), F32)],
-        [pltpu.VMEM((rows, width), BF16)] * 4 + [total, line(FIRST_CAP, wide), col_list] + [narrow] * 4 + window + [ids_in, row_list, col_list, row_list, col_list, row_list]
+        [pltpu.VMEM((rows, width), BF16)] * 4 + [total, line(FIRST_CAP, wide), col_list] + [narrow] * 4
+        + [pltpu.VMEM((4, WINDOW, width), BF16), pltpu.VMEM((rows, META), F32)]
+        + [pltpu.VMEM((4 * heads, 1, rows), F32)] * 2
+        + [ids_in, row_list, col_list, row_list, col_list, row_list]
         + [pltpu.VMEM((LINE * FIRST_CAP, wide + META), F32)]
         + [line(FIRST_CAP, wide + META)] * 2 + [line(NEXT_CAP, wide + META)] * 2
         + [pltpu.VMEM((LINE * NEXT_CAP, wide), F32)] + [line(NEXT_CAP, wide)] * 2 + [line(FIRST_CAP, wide)]
         + [pltpu.VMEM((1, LINE * FIRST_CAP), jnp.int32), pltpu.VMEM((pairs, 1, LINE * NEXT_CAP), jnp.int32)]
         + [pltpu.VMEM((2, 1, META), F32), pltpu.VMEM((peers - 1, 1, META), F32), pltpu.VMEM((owners, 1, META), F32)]
-        + sems + [dma((4,)), dma((4,)), dma((2, peers - 1)), dma, dma, dma((4,))],
+        + [dma((2, peers - 1)), dma((2, 4)), dma((2,))] + sems[3:] + [dma((4,)), dma((4,)), dma((2, peers - 1)), dma, dma, dma((4,))],
         0,
         [anywhere] * 4 + [vmem],
         [vmem] * 5,

time: 143 us -> 138 us (0.965)
  Pallas kernels: 141 us -> 136 us
    pallas_call x1, Pallas kernels: 139 us -> 134 us  [call(): pl.pallas_call(functools.partial(body, owners, peers, heads, rows), out_s...]
where the time goes in v3:
time: 138 us
  Pallas kernels  136 us (99%)
    pallas_call x1, Pallas kernels, call(): pl.pallas_call(functools.partial(body, owners, peers, heads, rows), out_s...  134 us

profile of v3, /device:TPU:1, one launch (start us, length us, event | category | flops | bytes accessed | tf_op | source)
XLA Modules:
  0.0 137.9 jit_solution(10167261130151694007)
XLA Ops:
  0.6 0.0 copy-start.4
  0.7 0.7 copy-done.4
  1.4 0.1 dynamic_update_slice.3.ids_ref
  1.5 0.0 copy-start
  1.5 0.0 copy-start.1
  1.5 0.0 copy-start.2
  1.5 0.0 copy-start.3
  1.5 134.2 %shard_map.84 = (bf16[256,1024]{1,0:T(8,128)(2,1)S(1)}, bf16[256,1024]{1,0:T(8,128)(2,1)S(1)}, bf16[256,1024]{1,0:T(8,128)(2,1)S(1)}, bf16[256,1024]{1,0:T(8,128)(2,1)S(1)}, f32[1,128]{1,0:T(1,128)S(1)}) custom-call(bf16[256,1024]{1,0:T(8,128)(2,1)} %q_hbm.1, bf16[256,1024]{1,0:T(8,128)(2,1)} %k_hbm.1, bf16[256,1024]{1,0:T(8,128)(2,1)} %v_hbm.1, ...), custom_call_target="tpu_custom_call" | custom-call | tf_op jit(solution)/shard_map/pallas_call | solution.py:735
  135.8 0.0 copy-done
  135.8 0.0 copy-done.1
  135.8 0.0 copy-done.2
  135.8 0.0 copy-done.3
  135.8 0.2 conditional.1
  136.0 1.8 %shard_map.85 = (bf16[256,1024]{1,0:T(8,128)(2,1)}, bf16[256,1024]{1,0:T(8,128)(2,1)}, bf16[256,1024]{1,0:T(8,128)(2,1)}, bf16[256,1024]{1,0:T(8,128)(2,1)}) custom-call(bf16[256,1024]{1,0:T(8,128)(2,1)S(1)} %get-tuple-element.41.refs_0_, bf16[256,1024]{1,0:T(8,128)(2,1)S(1)} %get-tuple-element.42.refs_1_, bf16[256,1024]{1,0:T(8,128)(2,1)S(1)} %get-tuple-element.43.refs_2_, ...), custom_call_target="tpu_custom_call" | custom-call | tf_op jit(solution)/shard_map/pallas_call | solution.py:782
  (1 shorter events, 0.0 us)
Async XLA Ops:
  0.6 0.7 copy-start.4
  1.5 134.3 %copy-start = (bf16[256,1024]{1,0:T(8,128)(2,1)S(1)}, bf16[256,1024]{1,0:T(8,128)(2,1)}, u32[]{:S(2)}) copy-start(bf16[256,1024]{1,0:T(8,128)(2,1)} %q_hbm.1) | copy-start | bytes 1572868
  1.5 134.3 %copy-start.1 = (bf16[256,1024]{1,0:T(8,128)(2,1)S(1)}, bf16[256,1024]{1,0:T(8,128)(2,1)}, u32[]{:S(2)}) copy-start(bf16[256,1024]{1,0:T(8,128)(2,1)} %k_hbm.1) | copy-start | bytes 1572868
  1.5 134.3 %copy-start.2 = (bf16[256,1024]{1,0:T(8,128)(2,1)S(1)}, bf16[256,1024]{1,0:T(8,128)(2,1)}, u32[]{:S(2)}) copy-start(bf16[256,1024]{1,0:T(8,128)(2,1)} %v_hbm.1) | copy-start | bytes 1572868
  1.5 134.3 %copy-start.3 = (bf16[256,1024]{1,0:T(8,128)(2,1)S(1)}, bf16[256,1024]{1,0:T(8,128)(2,1)}, u32[]{:S(2)}) copy-start(bf16[256,1024]{1,0:T(8,128)(2,1)} %g_hbm.1) | copy-start | bytes 1572868
